TPU v7x, 256 devices: a whole 4x4x8 slice. The times are simulated.
256 devices in a mesh: ew: 8 (over y, z_hi), ns: 32 (over z_lo, x, core).
Axes of the slice: x: 4, y: 4, z: 8 (z_hi: 2, z_lo: 4; z = z_hi * 4 + z_lo), core: 2. Of those that a mesh axis runs over, the one named last changes fastest.
Arguments:
- couplings: bfloat16 [8, 32, 16, 128, 2048], P('ew', 'ns'), may hold values from -0.125 to 0.125
- inverses: bfloat16 [8, 32, 16, 128, 128], P('ew', 'ns'), as said below
- pattern: int32 [8, 32, 16, 16], P('ew', 'ns'), may hold values 0 or 1
- counts: int32 [8, 32], P('ew', 'ns'), may hold values from 1 to 16, as said below
- basis: bfloat16 [8, 32, 128, 2048], P('ew', 'ns'), may hold values from -0.125 to 0.125
Outputs:
- south_front: float32 [8, 32, 768, 768], P('ew', 'ns')
- west_front: float32 [8, 32, 256, 256], P('ew', 'ns')
- coarse: float32 [8, 32, 128, 128], P('ew', 'ns')
Inputs may be any that keep to these rules, and one draw needn't show every extreme that they name: `counts`: some subdomain has exactly 16 live block columns. `inverses`: each block is symmetric.
All inputs are finite; a program needn't handle non-finite values. No bound on the sum of `pattern` on one device may be relied on, other than what follows from the above.
Results may differ from a plain program's by a relative error of at most 0.0015.
Values may be sent and summed in bfloat16 or wider, within the bound.
No kernel may reach another device: no remote copies, remote signals or barrier semaphores. Data moves between devices by JAX's collectives and lax.ppermute only.
A program may use at most 128 MiB of HBM per device.

v0:
```python
import jax
import jax.numpy as jnp
from jax import lax
from jax.sharding import PartitionSpec as P

B = 128
SN = 6
SE = 2


def from_behind(block, axis, distance):
    devices = range(lax.axis_size(axis))
    route = [(i - distance, i) for i in devices if i - distance in devices]
    return lax.ppermute(block, axis, route)


def solve_all(slabs, inverse):
    return jnp.einsum("kab,kbc->kac", inverse, slabs, preferred_element_type=jnp.float32).astype(
        jnp.bfloat16
    )


def edge_parts(slabs, solved, edges):
    results = []
    for edge in edges:
        slab = slabs[:, :, edge[0] : edge[0] + edge[1]]
        answer = solved[:, :, edge[0] : edge[0] + edge[1]]
        results.append(-jnp.einsum("kbi,kbj->ij", slab, answer, preferred_element_type=jnp.float32))
    return tuple(results)


def pass_edges(high_parts):
    from_west = from_behind(high_parts[0], "ew", 1)
    from_south = from_behind(high_parts[1], "ns", 1)
    return (from_west, from_south)


def shards(couplings, inverses, pattern, counts, basis):
    coupling = couplings[0, 0]
    inverse = inverses[0, 0]
    touched = pattern[0, 0]
    count = counts[0, 0]
    blocks_total = coupling.shape[0]
    north_start = SN * B
    west_start = 2 * SN * B
    east_start = west_start + SE * B
    south_edge = (0, SN * B)
    north_edge = (north_start, SN * B)
    west_edge = (west_start, SE * B)
    east_edge = (east_start, SE * B)
    columns = jnp.repeat(touched, B, axis=1)
    live = (jnp.arange(blocks_total, dtype=jnp.int32) < count).astype(jnp.int32)[:, None]
    keep = (columns * live).astype(jnp.bfloat16)
    masked = coupling * keep[:, None, :]
    high_edges = [east_edge, north_edge]
    solved = solve_all(masked, inverse)
    every_part = edge_parts(masked, solved, [south_edge, west_edge] + high_edges)
    low_parts = every_part[:2]
    from_west, from_south = pass_edges(every_part[2:])
    south_front = low_parts[0] + from_south
    west_front = low_parts[1] + from_west
    front_half = west_front.astype(jnp.bfloat16)
    row_basis = basis[0, 0]
    rank = row_basis.shape[0]
    edge_width = SE * B
    piece = lax.all_gather(front_half, "ew", axis=0, tiled=True)
    pieces = piece.shape[0] // edge_width
    columns_here = row_basis.reshape(rank, pieces, edge_width)
    fronts = piece.reshape(pieces, edge_width, edge_width)
    projected = jnp.einsum(
        "rnk,nkl->rnl", columns_here, fronts, preferred_element_type=jnp.float32
    ).astype(jnp.bfloat16)
    coarse = jnp.einsum("rnl,snl->rs", projected, columns_here, preferred_element_type=jnp.float32)
    return (south_front[None, None], west_front[None, None], coarse[None, None])


def solution(mesh):
    return jax.shard_map(
        shards,
        mesh=mesh,
        in_specs=(
            P("ew", "ns", None, None, None),
            P("ew", "ns", None, None, None),
            P("ew", "ns", None, None),
            P("ew", "ns"),
            P("ew", "ns", None, None),
        ),
        out_specs=(P("ew", "ns", None, None), P("ew", "ns", None, None), P("ew", "ns", None, None)),
        check_vma=False,
    )
```

profile of v0, /device:TPU:2, one launch (start us, length us, event | category | flops | bytes accessed | tf_op | source)
XLA Modules:
  0.0 137.7 jit_solution(6369991985110612012)
XLA Ops:
  7.2 0.0 copy-start
  7.2 0.0 copy-start.3
  7.2 0.0 all-gather.2.cloned.1.call-start
  7.2 12.3 %copy.8 = bf16[1,1,16,128,2048]{3,4,2,1,0:T(8,128)(2,1)} copy(bf16[1,1,16,128,2048]{4,3,2,1,0:T(8,128)(2,1)} %param.5) | data formatting | bytes 16777216 | tf_op args[0]
  20.2 0.0 copy-done.3
  20.3 0.1 broadcast_in_dim.14
  20.4 0.1 fusion.29
  20.4 6.4 %bitcast_multiply_fusion = bf16[16,128,2048]{1,2,0:T(8,128)(2,1)S(1)} fusion(bf16[1,1,16,128,2048]{3,4,2,1,0:T(8,128)(2,1)} %copy.8, bf16[16,2048]{1,0:T(8,128)(2,1)S(1)} %fusion.29), kind=kLoop, calls=%fused_computation | loop fusion | flops 4194304 | bytes 16842752 | tf_op jit(solution)/shard_map/mul | solution.py:54
  26.8 0.0 copy-done
  26.8 0.0 copy-start.1
  26.8 5.1 %convert_bitcast_fusion = bf16[16,128,2048]{1,2,0:T(8,128)(2,1)} fusion(bf16[16,128,2048]{1,2,0:T(8,128)(2,1)S(1)} %bitcast_multiply_fusion, bf16[1,1,16,128,128]{4,3,2,1,0:T(8,128)(2,1)S(1)} %copy-done), kind=kOutput, calls=%fused_computation.1 | convolution fusion | flops 1077936128 | bytes 17301504 | tf_op jit(solution)/shard_map/kab,kbc->kac/dot_general | solution.py:18
  31.9 2.0 %fusion.18 = f32[256,256]{1,0:T(8,128)S(1)} fusion(bf16[16,128,2048]{1,2,0:T(8,128)(2,1)} %convert_bitcast_fusion, bf16[16,128,2048]{1,2,0:T(8,128)(2,1)S(1)} %bitcast_multiply_fusion), kind=kOutput, calls=%fused_computation.16 | convolution fusion | flops 268500992 | bytes 2359296 | tf_op jit(solution)/shard_map/kbi,kbj->ij/dot_general | solution.py:28
  33.9 0.0 copy-start.2
  33.9 9.2 %collective-permute-start.1 = (f32[256,256]{1,0:T(8,128)S(1)}, f32[256,256]{1,0:T(8,128)S(1)}, u32[]{:S(2)}, u32[]{:S(2)}) collective-permute-start(f32[256,256]{1,0:T(8,128)S(1)} %fusion.18), channel_id=1, source_target_pairs={{0,32},{32,64},{64,96},{96,128},{128,160},{160,192},{192,224},{1,3... | collective-permute-start | bytes 786440 | tf_op jit(solution)/shard_map/ppermute | solution.py:14
  43.1 5.9 %bitcast_negate_fusion = f32[768,768]{1,0:T(8,128)} fusion(bf16[16,128,2048]{1,2,0:T(8,128)(2,1)} %convert_bitcast_fusion, bf16[16,128,2048]{1,2,0:T(8,128)(2,1)S(1)} %bitcast_multiply_fusion), kind=kOutput, calls=%fused_computation.8 | convolution fusion | flops 2416508928 | bytes 8650752 | tf_op jit(solution)/shard_map/kbi,kbj->ij/dot_general | solution.py:28
  49.1 1.9 %collective-permute-start = (f32[768,768]{1,0:T(8,128)}, f32[768,768]{1,0:T(8,128)}, u32[]{:S(2)}, u32[]{:S(2)}) collective-permute-start(f32[768,768]{1,0:T(8,128)} %bitcast_negate_fusion), channel_id=1, source_target_pairs={{0,1},{1,2},{2,3},{3,4},{4,5},{5,6},{6,7},{7,8},{8,9},{9,10},{10,1... | collective-permute-start | bytes 7077896 | tf_op jit(solution)/shard_map/ppermute | solution.py:14
  51.0 0.0 collective-permute-done.1
  51.0 2.4 %fusion.30 = (bf16[256,256]{1,0:T(8,128)(2,1)}, f32[256,256]{1,0:T(8,128)}) fusion(f32[256,256]{1,0:T(8,128)S(1)} %collective-permute-done.1, bf16[16,128,2048]{1,2,0:T(8,128)(2,1)} %convert_bitcast_fusion, bf16[16,128,2048]{1,2,0:T(8,128)(2,1)S(1)} %bitcast_multiply_fusion), kind=kOutput, calls=%fused_computation.30 | convolution fusion | flops 268632064 | bytes 2752512 | tf_op jit(solution)/shard_map/kbi,kbj->ij/dot_general | solution.py:28
  53.5 0.0 all-gather.2.cloned.1.call-update
  53.5 0.1 copy.20
  53.6 67.2 %all-gather.2.cloned.1.call-done = bf16[2048,256]{1,0:T(8,128)(2,1)} async-done(((bf16[256,256]{1,0:T(8,128)(2,1)}), bf16[2048,256]{1,0:T(8,128)(2,1)}) %all-gather.2.cloned.1.call-update) | async-done | bytes 1048592 | tf_op jit(solution)/shard_map/all_gather | solution.py:66
  120.8 2.4 %fusion.21 = f32[1,1,128,128]{3,2,1,0:T(8,128)} fusion(bf16[8,256,256]{2,1,0:T(8,128)(2,1)} %bitcast.57, bf16[128,8,256]{2,1,0:T(8,128)(2,1)S(1)} %bitcast.54), kind=kOutput, calls=%fused_computation.20 | convolution fusion | flops 201588736 | bytes 1638400 | tf_op jit(solution)/shard_map/rnl,snl->rs/dot_general | solution.py:73
  123.2 0.0 collective-permute-done
  123.2 7.6 %fusion.7 = f32[1,1,768,768]{3,2,1,0:T(8,128)} fusion(f32[768,768]{1,0:T(8,128)} %collective-permute-done, bf16[16,128,2048]{1,2,0:T(8,128)(2,1)} %convert_bitcast_fusion, bf16[16,128,2048]{1,2,0:T(8,128)(2,1)} %copy-done.1), kind=kOutput, calls=%fused_computation.11 | convolution fusion | flops 2417098752 | bytes 11010048 | tf_op jit(solution)/shard_map/kbi,kbj->ij/dot_general | solution.py:28
  (3 shorter events, 0.0 us)
Async XLA Ops:
  7.2 19.7 %copy-start = (bf16[1,1,16,128,128]{4,3,2,1,0:T(8,128)(2,1)S(1)}, bf16[1,1,16,128,128]{4,3,2,1,0:T(8,128)(2,1)}, u32[]{:S(2)}) copy-start(bf16[1,1,16,128,128]{4,3,2,1,0:T(8,128)(2,1)} %param.6) | copy-start | bytes 1572868
  7.2 13.1 %copy-start.3 = (s32[1,1,16,16]{3,2,1,0:T(8,128)S(1)}, s32[1,1,16,16]{3,2,1,0:T(8,128)}, u32[]{:S(2)}) copy-start(s32[1,1,16,16]{3,2,1,0:T(8,128)} %param.7) | copy-start | bytes 3076
  7.2 113.6 %all-gather.2.cloned.1.call-start = ((), (), s32[]{:S(2)}) async-start(), calls=%async_computation | async-start | bytes 1179648 | tf_op jit(solution)/shard_map/all_gather | solution.py:66
  26.8 24.2 %copy-start.1 = (bf16[16,128,2048]{1,2,0:T(8,128)(2,1)}, bf16[16,128,2048]{1,2,0:T(8,128)(2,1)S(1)}, u32[]{:S(2)}) copy-start(bf16[16,128,2048]{1,2,0:T(8,128)(2,1)S(1)} %bitcast_multiply_fusion) | copy-start | bytes 25165828
  33.9 19.6 %copy-start.2 = (bf16[1,1,128,2048]{3,2,1,0:T(8,128)(2,1)S(1)}, bf16[1,1,128,2048]{3,2,1,0:T(8,128)(2,1)}, u32[]{:S(2)}) copy-start(bf16[1,1,128,2048]{3,2,1,0:T(8,128)(2,1)} %param.9) | copy-start | bytes 1572868
  33.9 17.1 %collective-permute-start.1 = (f32[256,256]{1,0:T(8,128)S(1)}, f32[256,256]{1,0:T(8,128)S(1)}, u32[]{:S(2)}, u32[]{:S(2)}) collective-permute-start(f32[256,256]{1,0:T(8,128)S(1)} %fusion.18), channel_id=1, source_target_pairs={{0,32},{32,64},{64,96},{96,128},{128,160},{160,192},{192,224},{1,3... | collective-permute-start | bytes 786440 | tf_op jit(solution)/shard_map/ppermute | solution.py:14
  49.1 74.1 %collective-permute-start = (f32[768,768]{1,0:T(8,128)}, f32[768,768]{1,0:T(8,128)}, u32[]{:S(2)}, u32[]{:S(2)}) collective-permute-start(f32[768,768]{1,0:T(8,128)} %bitcast_negate_fusion), channel_id=1, source_target_pairs={{0,1},{1,2},{2,3},{3,4},{4,5},{5,6},{6,7},{7,8},{8,9},{9,10},{10,1... | collective-permute-start | bytes 7077896 | tf_op jit(solution)/shard_map/ppermute | solution.py:14
Sparse Core Ops, SparseCore 0:
  53.6 67.1 all-gather.1
where the time goes:
time: 138 us
  waiting for transfers between devices  67.2 us (49%)
  matrix products  25.4 us (18%)
  between operations  14.8 us (11%)
  local copies, waits for them, and re-layouts  12.6 us (9%)
  starting transfers between devices  11.2 us (8%)
  other arithmetic  6.46 us (5%)
    all_gather x1, waiting for transfers between devices, shards(): piece = lax.all_gather(front_half, 'ew', axis=0, tiled=True)  67.2 us
    dot_general x4, matrix products, edge_parts(): jnp.einsum('kbi,kbj->ij', slab, answer, preferred_element_type=jnp.float32)  17.9 us
    unnamed x10, local copies, waits for them, and re-layouts  12.5 us
    ppermute x2, starting transfers between devices, from_behind(): return lax.ppermute(block, axis, route)  11.2 us
    mul x1, other arithmetic, shards(): masked = coupling * keep[:, None, :]  6.38 us
    dot_general x1, matrix products, solve_all(): jnp.einsum('kab,kbc->kac', inverse, slabs, preferred_element_type=jnp.flo...  5.05 us
  transfers between devices with their start and end apart: 3, of which 1 were waited for; matrix products, arithmetic and copies ran while one was open for 8% of the time, Pallas kernels for 0%

commit v1 on v0

v1 whole, which is shorter than its diff:
```python
import functools

import jax
import jax.numpy as jnp
from jax import lax
from jax.experimental import pallas as pl
from jax.experimental.pallas import tpu as pltpu
from jax.sharding import PartitionSpec as P

B = 128
SN = 6
SE = 2
NS_W = SN * B
EW_W = SE * B
CHUNK = 4


def edges_kernel(first_block, edge, keep_ref, x_ref, inv_ref, *rest):
    outs, (m_ref, s_ref) = rest[:-2], rest[-2:]
    step = pl.program_id(0)
    width = x_ref.shape[-1]
    for kk in range(CHUNK):
        rows = slice(kk * B, (kk + 1) * B)
        for j in range(width // B):
            cols = slice(j * B, (j + 1) * B)
            keep = keep_ref[step * CHUNK + kk, first_block + j].astype(jnp.float32).astype(jnp.bfloat16)
            m_ref[rows, cols] = x_ref[0, 0, kk, :, cols] * keep
        solved = jnp.dot(inv_ref[0, 0, kk], m_ref[rows, :], preferred_element_type=jnp.float32)
        s_ref[rows, :] = solved.astype(jnp.bfloat16)
    for index, out in enumerate(outs):
        cols = slice(index * edge, (index + 1) * edge)
        part = lax.dot_general(
            m_ref[:, cols], s_ref[:, cols], (((0,), (0,)), ((), ())), preferred_element_type=jnp.float32
        )

        @pl.when(step == 0)
        def _():
            out[...] = -part

        @pl.when(step > 0)
        def _():
            out[...] = out[...] - part


def edges(name, coupling, inverse, keep, start, edge, count):
    blocks = coupling.shape[2]
    width = edge * count
    return pl.pallas_call(
        functools.partial(edges_kernel, start // B, edge),
        out_shape=[jax.ShapeDtypeStruct((edge, edge), jnp.float32)] * count,
        grid_spec=pltpu.PrefetchScalarGridSpec(
            num_scalar_prefetch=1,
            grid=(blocks // CHUNK,),
            in_specs=[
                pl.BlockSpec((1, 1, CHUNK, B, width), lambda c, keep: (0, 0, c, 0, start // width)),
                pl.BlockSpec((1, 1, CHUNK, B, B), lambda c, keep: (0, 0, c, 0, 0)),
            ],
            out_specs=[pl.BlockSpec((edge, edge), lambda c, keep: (0, 0))] * count,
            scratch_shapes=[
                pltpu.VMEM((CHUNK * B, width), jnp.bfloat16),
                pltpu.VMEM((CHUNK * B, width), jnp.bfloat16),
            ],
        ),
        cost_estimate=pl.CostEstimate(
            flops=2 * blocks * B * (B * width + edge * edge * count),
            transcendentals=0,
            bytes_accessed=2 * blocks * B * (width + B) + 4 * edge * edge * count,
        ),
        name=name,
    )(keep, coupling, inverse)


def from_behind(block, axis, distance):
    devices = range(lax.axis_size(axis))
    route = [(i - distance, i) for i in devices if i - distance in devices]
    return lax.ppermute(block, axis, route)


def ring(block, axis, distance):
    size = lax.axis_size(axis)
    return lax.ppermute(block, axis, [(i, (i + distance) % size) for i in range(size)])


def coarse_kernel(me_ref, q_ref, *refs):
    fronts, out_ref = refs[:-1], refs[-1]
    size = len(fronts)
    total = jnp.zeros(out_ref.shape, jnp.float32)
    for i in range(size):
        owner = lax.rem(me_ref[0] + size - 2 * (i // 2), size)
        if i % 2:
            owner = owner + 1 - 2 * lax.rem(owner, 2)
        q = q_ref[0, 0, :, pl.ds(pl.multiple_of(owner * EW_W, EW_W), EW_W)]
        projected = jnp.dot(q, fronts[i][...], preferred_element_type=jnp.float32).astype(jnp.bfloat16)
        total = total + lax.dot_general(
            projected, q, (((1,), (1,)), ((), ())), preferred_element_type=jnp.float32
        )
    out_ref[...] = total


def coarse_of(me, basis, fronts):
    rank = basis.shape[2]
    vmem = pl.BlockSpec(memory_space=pltpu.VMEM)
    return pl.pallas_call(
        coarse_kernel,
        out_shape=jax.ShapeDtypeStruct((rank, rank), jnp.float32),
        in_specs=[pl.BlockSpec(memory_space=pltpu.SMEM)] + [vmem] * (1 + len(fronts)),
        out_specs=vmem,
        name="coarse",
    )(me, basis, *fronts)


def shards(couplings, inverses, pattern, counts, basis):
    touched = pattern[0, 0]
    blocks = touched.shape[0]
    live = (jnp.arange(blocks, dtype=jnp.int32) < counts[0, 0]).astype(jnp.int32)[:, None]
    keep = touched * live
    west_start = 2 * NS_W
    west, east = edges("east_west", couplings, inverses, keep, west_start, EW_W, 2)
    with jax.named_scope("shift_east"):
        from_west = from_behind(east, "ew", 1)
    (north,) = edges("north", couplings, inverses, keep, NS_W, NS_W, 1)
    with jax.named_scope("shift_north"):
        from_south = from_behind(north, "ns", 1)
    west_front = west + from_west
    half = west_front.astype(jnp.bfloat16)
    size = lax.axis_size("ew")
    with jax.named_scope("across"):
        other = lax.ppermute(half, "ew", [(i, i ^ 1) for i in range(size)])
    with jax.named_scope("row_own"):
        own_row = [ring(half, "ew", d) for d in range(2, size, 2)]
    (south,) = edges("south", couplings, inverses, keep, 0, NS_W, 1)
    with jax.named_scope("row_other"):
        other_row = [ring(other, "ew", d) for d in range(2, size, 2)]
    fronts = []
    for pair in zip([half] + own_row, [other] + other_row):
        fronts.extend(pair)
    me = lax.axis_index("ew").astype(jnp.int32).reshape(1)
    coarse = coarse_of(me, basis, fronts)
    south_front = south + from_south
    return (south_front[None, None], west_front[None, None], coarse[None, None])


def solution(mesh):
    return jax.shard_map(
        shards,
        mesh=mesh,
        in_specs=(
            P("ew", "ns", None, None, None),
            P("ew", "ns", None, None, None),
            P("ew", "ns", None, None),
            P("ew", "ns"),
            P("ew", "ns", None, None),
        ),
        out_specs=(P("ew", "ns", None, None), P("ew", "ns", None, None), P("ew", "ns", None, None)),
        check_vma=False,
    )
```

time: 138 us -> 90.4 us (0.66)
  the two profiles are of different devices: /device:TPU:2 before, /device:TPU:71 now
where the time goes in v1:
time: 90.4 us; the launch traced here: 89.9 us
  waiting for transfers between devices  27.7 us (31%)
  starting transfers between devices  27.4 us (30%)
  Pallas kernels  26.3 us (29%)
  other arithmetic  6.42 us (7%)
  between operations  1.39 us (2%)
    ppermute x2, waiting for transfers between devices, from_behind(): return lax.ppermute(block, axis, route)  27.7 us
    pallas_call x3, Pallas kernels, edges(): pl.pallas_call(functools.partial(edges_kernel, start // B, edge), out_sha...  23.6 us
    ppermute x6, starting transfers between devices, ring(): lax.ppermute(block, axis, [(i, (i + distance) % size) for i in range(size)])  11.4 us
    ppermute x2, starting transfers between devices, from_behind(): return lax.ppermute(block, axis, route)  10.1 us
    ppermute x1, starting transfers between devices, shards(): other = lax.ppermute(half, 'ew', [(i, i ^ 1) for i in range(size)])  5.81 us
    broadcast_in_dim x1, other arithmetic, shards(): return (south_front[None, None], west_front[None, None], coarse[None, None])  3.36 us
    pallas_call x1, Pallas kernels, coarse_of(): pl.pallas_call(coarse_kernel, out_shape=jax.ShapeDtypeStruct((rank, rank)...  2.64 us
  transfers between devices with their start and end apart: 9, of which 1 were waited for; matrix products, arithmetic and copies ran while one was open for 2% of the time, Pallas kernels for 20%

profile of v1, /device:TPU:71, one launch (start us, length us, event | category | flops | bytes accessed | tf_op | source)
XLA Modules:
  0.0 89.9 jit_solution(7365916819460722307)
XLA Ops:
  1.3 1.4 %bitcast_multiply_fusion.keep_ref = s32[16,16]{1,0:T(8,128)} fusion(s32[1,1,16,16]{3,2,1,0:T(8,128)} %param.7, s32[16]{0:T(128)S(1)} %compare_convert_fusion), kind=kLoop, calls=%fused_computation.3 | loop fusion | flops 256 | bytes 2112 | tf_op jit(solution)/shard_map/mul | solution.py:116
  2.7 8.6 %north.1 = f32[768,768]{1,0:T(8,128)} custom-call(s32[16,16]{1,0:T(8,128)} %bitcast_multiply_fusion.keep_ref, bf16[1,1,16,128,2048]{4,3,2,1,0:T(8,128)(2,1)} %x_ref.5, bf16[1,1,16,128,128]{4,3,2,1,0:T(8,128)(2,1)} %inv_ref.5), custom_call_target="tpu_custom_call" | custom-call | flops 2818572288 | bytes 6029312 | tf_op jit(solution)/shard_map/north/pallas_call | solution.py:48
  11.3 4.0 %collective-permute-start = (f32[768,768]{1,0:T(8,128)}, f32[768,768]{1,0:T(8,128)S(1)}, u32[]{:S(2)}, u32[]{:S(2)}) collective-permute-start(f32[768,768]{1,0:T(8,128)} %north.1), channel_id=1, source_target_pairs={{0,1},{1,2},{2,3},{3,4},{4,5},{5,6},{6,7},{7,8},{8,9},{9,10},{10,1... | collective-permute-start | bytes 7077896 | tf_op jit(solution)/shard_map/shift_north/ppermute | solution.py:76
  15.3 6.3 %east_west.1 = (f32[256,256]{1,0:T(8,128)}, f32[256,256]{1,0:T(8,128)}) custom-call(s32[16,16]{1,0:T(8,128)} %bitcast_multiply_fusion.keep_ref, bf16[1,1,16,128,2048]{4,3,2,1,0:T(8,128)(2,1)} %x_ref.5, bf16[1,1,16,128,128]{4,3,2,1,0:T(8,128)(2,1)} %inv_ref.5), custom_call_target="tpu_custom_call" | custom-call | flops 805306368 | bytes 3145728 | tf_op jit(solution)/shard_map/east_west/pallas_call | solution.py:48
  21.6 6.1 %collective-permute-start.1 = (f32[256,256]{1,0:T(8,128)}, f32[256,256]{1,0:T(8,128)S(1)}, u32[]{:S(2)}, u32[]{:S(2)}) collective-permute-start(f32[256,256]{1,0:T(8,128)} %get-tuple-element.6), channel_id=1, source_target_pairs={{0,32},{32,64},{64,96},{96,128},{128,160},{160,192},{192,224},{1,3... | collective-permute-start | bytes 786440 | tf_op jit(solution)/shard_map/shift_east/ppermute | solution.py:76
  27.8 27.7 %collective-permute-done.1 = f32[256,256]{1,0:T(8,128)S(1)} collective-permute-done((f32[256,256]{1,0:T(8,128)}, f32[256,256]{1,0:T(8,128)S(1)}, u32[]{:S(2)}, u32[]{:S(2)}) %collective-permute-start.1) | collective-permute-done | bytes 262176 | tf_op jit(solution)/shard_map/shift_east/ppermute | solution.py:76
  55.4 1.7 %add_convert_fusion = (bf16[256,256]{1,0:T(8,128)(2,1)S(1)}, f32[1,1,256,256]{3,2,1,0:T(8,128)}) fusion(f32[256,256]{1,0:T(8,128)} %get-tuple-element.5, f32[256,256]{1,0:T(8,128)S(1)} %collective-permute-done.1), kind=kLoop, calls=%fused_computation.1 | loop fusion | flops 131072 | bytes 917504 | tf_op jit(solution)/shard_map/convert_element_type | solution.py:125
  57.1 5.8 %collective-permute-start.2 = (bf16[256,256]{1,0:T(8,128)(2,1)S(1)}, bf16[256,256]{1,0:T(8,128)(2,1)S(1)}, u32[]{:S(2)}, u32[]{:S(2)}) collective-permute-start(bf16[256,256]{1,0:T(8,128)(2,1)S(1)} %get-tuple-element.7.refs_0_), channel_id=1, source_target_pairs={{0,32},{32,0},{64,96},{96,64},{128,160},{160,128},{192,224},{224,1... | collective-permute-start | bytes 393224 | tf_op jit(solution)/shard_map/across/ppermute | solution.py:128
  62.9 1.2 %collective-permute-start.3 = (bf16[256,256]{1,0:T(8,128)(2,1)S(1)}, bf16[256,256]{1,0:T(8,128)(2,1)S(1)}, u32[]{:S(2)}, u32[]{:S(2)}) collective-permute-start(bf16[256,256]{1,0:T(8,128)(2,1)S(1)} %get-tuple-element.7.refs_0_), channel_id=1, source_target_pairs={{0,64},{32,96},{64,128},{96,160},{128,192},{160,224},{192,0},{224,... | collective-permute-start | bytes 393224 | tf_op jit(solution)/shard_map/row_own/ppermute | solution.py:81
  64.1 2.6 %collective-permute-start.5 = (bf16[256,256]{1,0:T(8,128)(2,1)S(1)}, bf16[256,256]{1,0:T(8,128)(2,1)S(1)}, u32[]{:S(2)}, u32[]{:S(2)}) collective-permute-start(bf16[256,256]{1,0:T(8,128)(2,1)S(1)} %get-tuple-element.7.refs_0_), channel_id=1, source_target_pairs={{0,128},{32,160},{64,192},{96,224},{128,0},{160,32},{192,64},{224,... | collective-permute-start | bytes 393224 | tf_op jit(solution)/shard_map/row_own/ppermute | solution.py:81
  66.7 1.1 %collective-permute-start.7 = (bf16[256,256]{1,0:T(8,128)(2,1)S(1)}, bf16[256,256]{1,0:T(8,128)(2,1)S(1)}, u32[]{:S(2)}, u32[]{:S(2)}) collective-permute-start(bf16[256,256]{1,0:T(8,128)(2,1)S(1)} %get-tuple-element.7.refs_0_), channel_id=1, source_target_pairs={{0,192},{32,224},{64,0},{96,32},{128,64},{160,96},{192,128},{224,1... | collective-permute-start | bytes 393224 | tf_op jit(solution)/shard_map/row_own/ppermute | solution.py:81
  67.8 0.0 collective-permute-done.2.refs_1_
  67.8 2.8 %collective-permute-start.4 = (bf16[256,256]{1,0:T(8,128)(2,1)S(1)}, bf16[256,256]{1,0:T(8,128)(2,1)S(1)}, u32[]{:S(2)}, u32[]{:S(2)}) collective-permute-start(bf16[256,256]{1,0:T(8,128)(2,1)S(1)} %collective-permute-done.2.refs_1_), channel_id=1, source_target_pairs={{0,64},{32,96},{64,128},{96,160},{128,192},{160,224},{192,0},{224,... | collective-permute-start | bytes 393224 | tf_op jit(solution)/shard_map/row_other/ppermute | solution.py:81
  70.7 2.9 %collective-permute-start.6 = (bf16[256,256]{1,0:T(8,128)(2,1)S(1)}, bf16[256,256]{1,0:T(8,128)(2,1)S(1)}, u32[]{:S(2)}, u32[]{:S(2)}) collective-permute-start(bf16[256,256]{1,0:T(8,128)(2,1)S(1)} %collective-permute-done.2.refs_1_), channel_id=1, source_target_pairs={{0,128},{32,160},{64,192},{96,224},{128,0},{160,32},{192,64},{224,... | collective-permute-start | bytes 393224 | tf_op jit(solution)/shard_map/row_other/ppermute | solution.py:81
  73.6 0.0 collective-permute-done.5.refs_4_
  73.6 0.8 collective-permute-start.8
  74.4 8.6 %south.1 = f32[768,768]{1,0:T(8,128)} custom-call(s32[16,16]{1,0:T(8,128)} %bitcast_multiply_fusion.keep_ref, bf16[1,1,16,128,2048]{4,3,2,1,0:T(8,128)(2,1)} %x_ref.5, bf16[1,1,16,128,128]{4,3,2,1,0:T(8,128)(2,1)} %inv_ref.5), custom_call_target="tpu_custom_call" | custom-call | flops 2818572288 | bytes 6029312 | tf_op jit(solution)/shard_map/south/pallas_call | solution.py:48
  83.1 0.0 collective-permute-done.4.refs_3_
  83.1 0.6 copy-done.4
  83.7 0.1 copy-done.5
  83.8 0.0 copy-done.6
  83.8 0.0 copy-done.7
  83.8 2.6 %coarse.1 = f32[128,128]{1,0:T(8,128)} custom-call(s32[1]{0:T(128)} %bitcast.4.me_ref, bf16[1,1,128,2048]{3,2,1,0:T(8,128)(2,1)} %q_ref.1, bf16[256,256]{1,0:T(8,128)(2,1)} %copy-done, bf16[256,256]{1,0:T(8,128)(2,1)} %copy-done.1, bf16[256,256]{1,0:T(8,128)(2,1)} %copy-done.2, bf16[256,256]{1,0:T(8,128)(2,1)} %copy-done.5, bf16[256,256]{1,0:T(8,128)(2,1)} %copy-done.3, ...), custom_call_target="tpu_custom_call" | custom-call | tf_op jit(solution)/shard_map/coarse/pallas_call | solution.py:103
  86.5 3.4 %add_bitcast_fusion = f32[1,1,768,768]{3,2,1,0:T(8,128)} fusion(f32[768,768]{1,0:T(8,128)} %south.1, f32[768,768]{1,0:T(8,128)S(1)} %collective-permute-done), kind=kLoop, calls=%fused_computation | loop fusion | flops 589824 | bytes 7077888 | tf_op jit(solution)/shard_map/broadcast_in_dim | solution.py:140
  (18 shorter events, 0.0 us)
Async XLA Ops:
  11.3 75.2 %collective-permute-start = (f32[768,768]{1,0:T(8,128)}, f32[768,768]{1,0:T(8,128)S(1)}, u32[]{:S(2)}, u32[]{:S(2)}) collective-permute-start(f32[768,768]{1,0:T(8,128)} %north.1), channel_id=1, source_target_pairs={{0,1},{1,2},{2,3},{3,4},{4,5},{5,6},{6,7},{7,8},{8,9},{9,10},{10,1... | collective-permute-start | bytes 7077896 | tf_op jit(solution)/shard_map/shift_north/ppermute | solution.py:76
  21.6 33.8 %collective-permute-start.1 = (f32[256,256]{1,0:T(8,128)}, f32[256,256]{1,0:T(8,128)S(1)}, u32[]{:S(2)}, u32[]{:S(2)}) collective-permute-start(f32[256,256]{1,0:T(8,128)} %get-tuple-element.6), channel_id=1, source_target_pairs={{0,32},{32,64},{64,96},{96,128},{128,160},{160,192},{192,224},{1,3... | collective-permute-start | bytes 786440 | tf_op jit(solution)/shard_map/shift_east/ppermute | solution.py:76
  57.1 25.9 %copy-start = (bf16[256,256]{1,0:T(8,128)(2,1)}, bf16[256,256]{1,0:T(8,128)(2,1)S(1)}, u32[]{:S(2)}) copy-start(bf16[256,256]{1,0:T(8,128)(2,1)S(1)} %get-tuple-element.7.refs_0_) | copy-start | bytes 393220
  57.1 10.7 %collective-permute-start.2 = (bf16[256,256]{1,0:T(8,128)(2,1)S(1)}, bf16[256,256]{1,0:T(8,128)(2,1)S(1)}, u32[]{:S(2)}, u32[]{:S(2)}) collective-permute-start(bf16[256,256]{1,0:T(8,128)(2,1)S(1)} %get-tuple-element.7.refs_0_), channel_id=1, source_target_pairs={{0,32},{32,0},{64,96},{96,64},{128,160},{160,128},{192,224},{224,1... | collective-permute-start | bytes 393224 | tf_op jit(solution)/shard_map/across/ppermute | solution.py:128
  62.9 7.7 %collective-permute-start.3 = (bf16[256,256]{1,0:T(8,128)(2,1)S(1)}, bf16[256,256]{1,0:T(8,128)(2,1)S(1)}, u32[]{:S(2)}, u32[]{:S(2)}) collective-permute-start(bf16[256,256]{1,0:T(8,128)(2,1)S(1)} %get-tuple-element.7.refs_0_), channel_id=1, source_target_pairs={{0,64},{32,96},{64,128},{96,160},{128,192},{160,224},{192,0},{224,... | collective-permute-start | bytes 393224 | tf_op jit(solution)/shard_map/row_own/ppermute | solution.py:81
  64.1 9.5 %collective-permute-start.5 = (bf16[256,256]{1,0:T(8,128)(2,1)S(1)}, bf16[256,256]{1,0:T(8,128)(2,1)S(1)}, u32[]{:S(2)}, u32[]{:S(2)}) collective-permute-start(bf16[256,256]{1,0:T(8,128)(2,1)S(1)} %get-tuple-element.7.refs_0_), channel_id=1, source_target_pairs={{0,128},{32,160},{64,192},{96,224},{128,0},{160,32},{192,64},{224,... | collective-permute-start | bytes 393224 | tf_op jit(solution)/shard_map/row_own/ppermute | solution.py:81
  66.7 16.3 %collective-permute-start.7 = (bf16[256,256]{1,0:T(8,128)(2,1)S(1)}, bf16[256,256]{1,0:T(8,128)(2,1)S(1)}, u32[]{:S(2)}, u32[]{:S(2)}) collective-permute-start(bf16[256,256]{1,0:T(8,128)(2,1)S(1)} %get-tuple-element.7.refs_0_), channel_id=1, source_target_pairs={{0,192},{32,224},{64,0},{96,32},{128,64},{160,96},{192,128},{224,1... | collective-permute-start | bytes 393224 | tf_op jit(solution)/shard_map/row_own/ppermute | solution.py:81
  67.8 15.2 %copy-start.1 = (bf16[256,256]{1,0:T(8,128)(2,1)}, bf16[256,256]{1,0:T(8,128)(2,1)S(1)}, u32[]{:S(2)}) copy-start(bf16[256,256]{1,0:T(8,128)(2,1)S(1)} %collective-permute-done.2.refs_1_) | copy-start | bytes 393220
  67.8 15.2 %collective-permute-start.4 = (bf16[256,256]{1,0:T(8,128)(2,1)S(1)}, bf16[256,256]{1,0:T(8,128)(2,1)S(1)}, u32[]{:S(2)}, u32[]{:S(2)}) collective-permute-start(bf16[256,256]{1,0:T(8,128)(2,1)S(1)} %collective-permute-done.2.refs_1_), channel_id=1, source_target_pairs={{0,64},{32,96},{64,128},{96,160},{128,192},{160,224},{192,0},{224,... | collective-permute-start | bytes 393224 | tf_op jit(solution)/shard_map/row_other/ppermute | solution.py:81
  70.7 12.3 %copy-start.2 = (bf16[256,256]{1,0:T(8,128)(2,1)}, bf16[256,256]{1,0:T(8,128)(2,1)S(1)}, u32[]{:S(2)}) copy-start(bf16[256,256]{1,0:T(8,128)(2,1)S(1)} %collective-permute-done.3.refs_2_) | copy-start | bytes 393220
  70.7 12.4 %collective-permute-start.6 = (bf16[256,256]{1,0:T(8,128)(2,1)S(1)}, bf16[256,256]{1,0:T(8,128)(2,1)S(1)}, u32[]{:S(2)}, u32[]{:S(2)}) collective-permute-start(bf16[256,256]{1,0:T(8,128)(2,1)S(1)} %collective-permute-done.2.refs_1_), channel_id=1, source_target_pairs={{0,128},{32,160},{64,192},{96,224},{128,0},{160,32},{192,64},{224,... | collective-permute-start | bytes 393224 | tf_op jit(solution)/shard_map/row_other/ppermute | solution.py:81
  73.6 9.4 %copy-start.3 = (bf16[256,256]{1,0:T(8,128)(2,1)}, bf16[256,256]{1,0:T(8,128)(2,1)S(1)}, u32[]{:S(2)}) copy-start(bf16[256,256]{1,0:T(8,128)(2,1)S(1)} %collective-permute-done.5.refs_4_) | copy-start | bytes 393220
  73.6 9.5 %collective-permute-start.8 = (bf16[256,256]{1,0:T(8,128)(2,1)S(1)}, bf16[256,256]{1,0:T(8,128)(2,1)S(1)}, u32[]{:S(2)}, u32[]{:S(2)}) collective-permute-start(bf16[256,256]{1,0:T(8,128)(2,1)S(1)} %collective-permute-done.2.refs_1_), channel_id=1, source_target_pairs={{0,192},{32,224},{64,0},{96,32},{128,64},{160,96},{192,128},{224,1... | collective-permute-start | bytes 393224 | tf_op jit(solution)/shard_map/row_other/ppermute | solution.py:81
  83.1 0.7 copy-start.4
  83.1 0.7 copy-start.5
  83.1 0.7 copy-start.6
  83.1 0.7 copy-start.7
